TPU v7x, 32 devices: a whole 2x2x4 slice. The times are simulated.
32 devices in a mesh: rows: 8 (over z, x), feat: 4 (over y, core).
Axes of the slice: x: 2, y: 2, z: 4, core: 2. Of those that a mesh axis runs over, the one named last changes fastest.
Arguments:
- features: float32 [16384, 1024], P('rows', 'feat')
- norm_gain: float32 [1024], P('feat'), may hold values from 0.1 to 1.9
- row_counts: int32 [8, 16], P('rows'), may hold values from 1 to 43, 86 in all within a row
- tile_cols: int32 [688], P('rows'), may hold values from 0 to 127, as said below
- tile_values: float32 [688, 128, 128], P('rows'), may hold values from -0.1875 to 0.1875
Outputs:
- normed: float32 [16384, 1024], P('rows', 'feat')
Inputs may be any that keep to these rules, and one draw needn't show every extreme that they name: `tile_cols`: node n lies in stripe n // 2048. There are exactly 3 heavy stripes; every device's tiles reference every block of every heavy stripe and every block of its own stripe. Every other block that a device's tiles reference is referenced by one of its tiles only, lies in no heavy stripe, and no two such blocks of one device lie in the same stripe; each device has exactly 3 such blocks. `row_counts`: each device's counts sum to 86.
All inputs are finite; a program needn't handle non-finite values.
Results may differ from a plain program's by a relative error of at most 0.0003.
Values sent between devices are 32-bit elements; how exact they have to be, the bound alone decides.
No kernel may reach another device: no remote copies, remote signals or barrier semaphores. Data moves between devices by JAX's collectives and lax.ppermute only.
A program may use at most 128 MiB of HBM per device.

v0:
```python
import jax
import jax.numpy as jnp
from jax import lax
from jax.sharding import PartitionSpec as P

HEAVY = 3


def broadcast(block, axis, owner):
    block = jnp.where(lax.axis_index(axis) == owner, block, jnp.zeros_like(block))
    return lax.psum(block, axis)


def per_device(features, norm_gain, row_counts, tile_cols, tile_values):
    node_dev, feat_dev = features.shape
    block_rows = tile_values.shape[1]
    blocks_dev = node_dev // block_rows
    tile_total = tile_values.shape[0]
    heavy_count = HEAVY
    devices = lax.axis_size("rows")
    my_index = lax.axis_index("rows")
    activated = jnp.maximum(features, 0.0)
    act_blocks = activated.reshape(blocks_dev, block_rows, feat_dev)
    owner_dev = tile_cols // blocks_dev
    local_block = tile_cols % blocks_dev
    is_own = owner_dev == my_index
    peer_ids = jnp.arange(devices, dtype=jnp.int32)
    block_ids = jnp.arange(blocks_dev, dtype=jnp.int32)
    to_peer = (owner_dev[None, :] == peer_ids[:, None]) & jnp.logical_not(is_own)[None, :]
    block_hit = jnp.any(
        to_peer[:, None, :] & (local_block[None, None, :] == block_ids[None, :, None]), axis=2
    )
    seen_count = jnp.sum(block_hit.astype(jnp.int32), axis=1)
    local_mark = (seen_count >= 2).astype(jnp.int32)
    heavy_mark = lax.pmax(local_mark, "rows")
    heavy_rank = jnp.cumsum(heavy_mark, dtype=jnp.int32) - 1
    heavy_list = []
    for stripe in range(heavy_count):
        heavy_list.append(
            jnp.sum(jnp.where((heavy_mark > 0) & (heavy_rank == stripe), peer_ids, 0))
        )
    heavy_ids = jnp.stack(heavy_list)
    stripes = []
    for stripe in range(heavy_count):
        stripes.append(broadcast(activated, "rows", heavy_ids[stripe]))
    heavy_blocks = jnp.stack(stripes).reshape(heavy_count * blocks_dev, block_rows, feat_dev)
    match_heavy = owner_dev[:, None] == heavy_ids[None, :]
    is_heavy = jnp.any(match_heavy, axis=1) & jnp.logical_not(is_own)
    stripe_ids = jnp.arange(heavy_count, dtype=jnp.int32)
    heavy_slot = (
        jnp.sum(match_heavy.astype(jnp.int32) * stripe_ids[None, :], axis=1) * blocks_dev
        + local_block
    )
    is_light = jnp.logical_not(is_own | is_heavy)
    to_owner = is_light[None, :] & (owner_dev[None, :] == peer_ids[:, None])
    wanted = jnp.max(jnp.where(to_owner, local_block[None, :], -1), axis=1)
    requested = lax.all_to_all(
        wanted.reshape(devices, 1), "rows", split_axis=0, concat_axis=0, tiled=True
    )[:, 0]
    request_valid = requested >= 0
    served = act_blocks[jnp.maximum(requested, 0)]
    outgoing = jnp.where(request_valid[:, None, None], served, 0.0)
    tile_counts = row_counts[0]
    row_ends = jnp.cumsum(tile_counts, dtype=jnp.int32)
    tile_index = jnp.arange(tile_total, dtype=jnp.int32)
    tile_row = jnp.sum((row_ends[None, :] <= tile_index[:, None]).astype(jnp.int32), axis=1)
    row_ids = jnp.arange(blocks_dev, dtype=jnp.int32)
    tile_of_owner = jnp.max(jnp.where(to_owner, tile_index[None, :], -1), axis=1)
    has_light = tile_of_owner >= 0
    light_tile = jnp.maximum(tile_of_owner, 0)
    light_values = jnp.where(has_light[:, None, None], tile_values[light_tile], 0.0)
    light_row = tile_row[light_tile]
    light_onehot = ((light_row[None, :] == row_ids[:, None]) & has_light[None, :]).astype(
        jnp.float32
    )
    piece = lax.all_to_all(outgoing, "rows", split_axis=0, concat_axis=0, tiled=True)
    width = piece.shape[2]
    partial_value = jnp.einsum("nij,njf->nif", light_values, piece, precision=lax.Precision.HIGHEST)
    summed = jnp.dot(
        light_onehot,
        partial_value.reshape(devices, block_rows * width),
        precision=lax.Precision.HIGHEST,
        preferred_element_type=jnp.float32,
    )
    light_sum = summed.reshape(node_dev, width)
    light_need = (devices - heavy_count - 1) * 3 // 4
    near_count = tile_total - light_need
    ranking = jnp.argsort(is_light.astype(jnp.int32), stable=True)[:near_count]
    near_panel = jnp.concatenate([heavy_blocks, act_blocks], axis=0)
    near_slot = jnp.where(is_own, heavy_count * blocks_dev + local_block, heavy_slot)[ranking]
    picked = near_panel[near_slot]
    products = jnp.einsum(
        "tij,tjf->tif", tile_values[ranking], picked, precision=lax.Precision.HIGHEST
    )
    near_onehot = (tile_row[ranking][None, :] == row_ids[:, None]).astype(jnp.float32)
    near_sum = jnp.dot(
        near_onehot,
        products.reshape(near_count, block_rows * feat_dev),
        precision=lax.Precision.HIGHEST,
        preferred_element_type=jnp.float32,
    )
    aggregate = near_sum.reshape(node_dev, feat_dev) + light_sum
    square_sum = lax.psum(jnp.sum(aggregate * aggregate, axis=1), "feat")
    mean_square = square_sum / (feat_dev * lax.axis_size("feat"))
    return aggregate * norm_gain[None, :] * lax.rsqrt(mean_square + 1e-05)[:, None]


def solution(mesh):
    placed = (P("rows", "feat"), P("feat"), P("rows", None), P("rows"), P("rows", None, None))
    return jax.shard_map(
        per_device, mesh=mesh, in_specs=placed, out_specs=P("rows", "feat"), check_vma=False
    )
```

profile of v0, /device:TPU:0, one launch (start us, length us, event | category | flops | bytes accessed | tf_op | source)
XLA Modules:
  0.0 341.9 jit_solution(11381033158909850786)
XLA Ops:
  8.2 13.1 %pmax.7 = s32[8]{0:T(128)S(1)} all-reduce(s32[8]{0:T(128)S(1)} %compare_convert_fusion), channel_id=1, replica_groups=mesh['rows'=8,'feat'=4] {'rows'}, use_global_device_ids=true, to_apply=%region_4.5 | all-reduce | flops 8 | bytes 64 | tf_op jit(solution)/shard_map/pmax | solution.py:35
  24.2 4.6 %select_bitcast_fusion.2 = (f32[1,2048,256]{2,1,0:T(8,128)}, f32[1,2048,256]{2,1,0:T(8,128)}, f32[1,2048,256]{2,1,0:T(8,128)}, f32[2048,256]{1,0:T(8,128)S(1)}) fusion(pred[]{:T(512)S(6)} %eq.136, f32[2048,256]{1,0:T(8,128)} %param.5, pred[]{:T(512)S(6)} %eq.137, pred[]{:T(512)S(6)} %eq.138), kind=kLoop, calls=%fused_computation.14 | loop fusion | flops 2097152 | bytes 10485763 | tf_op jit(solution)/shard_map/stack | solution.py:46
  28.8 2.0 pad_add_fusion
  31.1 9.3 %all_to_all.14 = s32[8,1,1]{2,1,0:T(1,128)S(1)} all-to-all(s32[8,1,1]{2,1,0:T(1,128)S(1)} %copy.13), channel_id=1, replica_groups=mesh['rows'=8,'feat'=4] {'rows'}, dimensions={0} | all-to-all | bytes 64 | tf_op jit(solution)/shard_map/all_to_all | solution.py:57
  42.7 3.6 %all-to-all-start.1 = ((f32[8,128,256]{2,1,0:T(8,128)}), f32[8,128,256]{2,1,0:T(8,128)S(1)}, u32[]{:S(2)}, u32[]{:S(2)}) async-start(f32[8,128,256]{2,1,0:T(8,128)} %broadcast_select_fusion), calls=%async_computation.1 | async-start | bytes 2097152 | tf_op jit(solution)/shard_map/all_to_all | solution.py:76
  46.5 2.6 sort.17
  51.1 4.0 %gather_fusion.5 = f32[8,128,128]{2,1,0:T(8,128)} fusion(f32[86,128,128]{2,1,0:T(8,128)} %param.9, s32[1024]{0:T(1024)S(1)} %pad_clamp_fusion.1), kind=kCustom, calls=%fused_computation.5 | custom fusion | bytes 1048608 | tf_op jit(solution)/shard_map/gather | solution.py:71
  55.1 5.9 %gather_fusion.1 = f32[83,128,128]{2,1,0:T(8,128)} fusion(f32[86,128,128]{2,1,0:T(8,128)} %param.9, s32[1024]{0:T(1024)S(1)} %pad_clamp_fusion.3), kind=kCustom, calls=%fused_computation.1 | custom fusion | bytes 10879308 | tf_op jit(solution)/shard_map/gather | solution.py:93
  61.1 1.2 gather_fusion.2
  62.4 35.4 %all-to-all-done.1 = f32[8,128,256]{2,1,0:T(8,128)S(1)} async-done(((f32[8,128,256]{2,1,0:T(8,128)}), f32[8,128,256]{2,1,0:T(8,128)S(1)}, u32[]{:S(2)}, u32[]{:S(2)}) %all-to-all-start.1) | async-done | bytes 1048608 | tf_op jit(solution)/shard_map/all_to_all | solution.py:76
  97.8 2.1 convolution_bitcast_fusion
  99.9 1.7 copy.15
  101.6 158.5 %all-reduce.3.cloned.1.call-done = (f32[1,2048,256]{2,1,0:T(8,128)}, f32[1,2048,256]{2,1,0:T(8,128)}, f32[1,2048,256]{2,1,0:T(8,128)}) async-done(((f32[1,2048,256]{2,1,0:T(8,128)}, f32[1,2048,256]{2,1,0:T(8,128)}, f32[1,2048,256]{2,1,0:T(8,128)}), (f32[1,2048,256]{2,1,0:T(8,128)}, f32[1,2048,256]{2,1,0:T(8,128)}, f32[1,2048,256]{2,1,0:T(8,128)})) %all-reduce.3.cloned.1.call-update) | async-done | bytes 6291472 | tf_op jit(solution)/shard_map/psum | solution.py:11
  260.0 3.3 pad_maximum_fusion.1
  263.3 3.9 %pad_maximum_fusion = f32[64,128,256]{2,1,0:T(8,128)} fusion(f32[16,128,256]{2,1,0:T(8,128)S(1)} %bitcast.51, f32[48,128,256]{2,1,0:T(8,128)S(1)} %bitcast.49), kind=kLoop, calls=%fused_computation.8 | loop fusion | flops 2097152 | bytes 16777216 | tf_op jit(solution)/shard_map/concatenate | solution.py:89
  267.2 11.7 %gather_fusion.3 = f32[83,128,256]{2,1,0:T(8,128)} fusion(f32[64,128,256]{2,1,0:T(8,128)} %pad_maximum_fusion, s32[1024]{0:T(1024)S(1)} %pad_clamp_fusion.2), kind=kCustom, calls=%fused_computation.3 | custom fusion | bytes 21758284 | tf_op jit(solution)/shard_map/gather | solution.py:91
  278.8 15.2 %fusion.22 = f32[83,128,256]{2,1,0:T(8,128)S(1)} fusion(f32[83,128,128]{2,1,0:T(8,128)} %gather_fusion.1, f32[83,128,256]{2,1,0:T(8,128)} %gather_fusion.3), kind=kOutput, calls=%fused_computation.77 | convolution fusion | flops 4177526784 | bytes 27197440 | tf_op jit(solution)/shard_map/tij,tjf->tif/dot_general | solution.py:92
  294.0 5.5 %pad.15 = f32[88,128,256]{2,1,0:T(8,128)} pad(f32[83,128,256]{2,1,0:T(8,128)S(1)} %fusion.22, f32[]{:T(128)} %constant.66.clone.1), padding=0_5x0_0x0_0 | pad | bytes 22413316
  299.5 16.1 %copy.14 = f32[11,8,128,256]{3,1,2,0:T(8,128)} copy(f32[11,8,128,256]{3,2,1,0:T(8,128)} %bitcast.47) | data formatting | bytes 23068672
  315.7 6.9 %fusion.3 = f32[16,32768]{1,0:T(8,128)S(1)} fusion(f32[83,32768]{1,0:T(8,128)} %bitcast.48, s32[83]{0:T(128)S(1)} %gather_fusion), kind=kOutput, calls=%fused_computation.29 | convolution fusion | flops 522192192 | bytes 12976460 | tf_op jit(solution)/shard_map/dot_general | solution.py:96
  322.6 2.4 convolution_add_fusion
  325.0 1.7 add.67
  327.1 6.4 %psum.31 = f32[2048]{0:T(1024)S(1)} all-reduce(f32[2048]{0:T(1024)S(1)} %multiply_reduce_fusion), channel_id=1, replica_groups=mesh['rows'=8,'feat'=4] {'feat'}, use_global_device_ids=true, to_apply=%region_18.19 | all-reduce | flops 2048 | bytes 16384 | tf_op jit(solution)/shard_map/psum | solution.py:103
  333.4 1.7 multiply_multiply_fusion
  (46 shorter events, 7.9 us)
Async XLA Ops:
  6.5 253.5 %all-reduce.3.cloned.1.call-start = ((), (), s32[]{:S(2)}) async-start(), calls=%async_computation.2 | async-start | bytes 12582912 | tf_op jit(solution)/shard_map/psum | solution.py:11
  28.8 17.5 %copy-start.3 = (s32[1,16]{1,0:T(1,128)S(1)}, s32[1,16]{1,0:T(1,128)}, u32[]{:S(2)}) copy-start(s32[1,16]{1,0:T(1,128)} %param.7) | copy-start | bytes 196
  42.7 55.0 %all-to-all-start.1 = ((f32[8,128,256]{2,1,0:T(8,128)}), f32[8,128,256]{2,1,0:T(8,128)S(1)}, u32[]{:S(2)}, u32[]{:S(2)}) async-start(f32[8,128,256]{2,1,0:T(8,128)} %broadcast_select_fusion), calls=%async_computation.1 | async-start | bytes 2097152 | tf_op jit(solution)/shard_map/all_to_all | solution.py:76
  55.1 6.0 %copy-start.1 = (s32[86]{0:T(128)S(1)}, s32[86]{0:T(128)}, u32[]{:S(2)}) copy-start(s32[86]{0:T(128)} %param.8) | copy-start | bytes 1036
  315.7 6.9 %copy-start = (f32[1,8,128,256]{3,1,2,0:T(8,128)S(1)}, f32[1,8,128,256]{3,1,2,0:T(8,128)}, u32[]{:S(2)}) copy-start(f32[1,8,128,256]{3,1,2,0:T(8,128)} %copy.15) | copy-start | bytes 3145732
  322.6 10.8 %copy-start.2 = (f32[256]{0:T(256)S(1)}, f32[256]{0:T(256)}, u32[]{:S(2)}) copy-start(f32[256]{0:T(256)} %param.6) | copy-start | bytes 3076
Sparse Core Ops, SparseCore 0:
  29.0 231.0 all-reduce.2
where the time goes:
time: 342 us
  waiting for transfers between devices  194 us (57%)
  local copies, waits for them, and re-layouts  50.5 us (15%)
  blocking collectives  28.8 us (8%)
  matrix products  26.6 us (8%)
  other arithmetic  23.2 us (7%)
  between operations  15.5 us (5%)
  starting transfers between devices  3.56 us (1%)
    psum x1, waiting for transfers between devices, broadcast(): return lax.psum(block, axis)  158 us
    all_to_all x1, waiting for transfers between devices, per_device(): lax.all_to_all(outgoing, 'rows', split_axis=0, concat_axis=0, tiled=True)  35.4 us
    unnamed x11, local copies, waits for them, and re-layouts  23.3 us
    dot_general x1, matrix products, per_device(): jnp.einsum('tij,tjf->tif', tile_values[ranking], picked, precision=lax.Pr...  15.2 us
    pmax x1, blocking collectives, per_device(): heavy_mark = lax.pmax(local_mark, 'rows')  13.1 us
    gather x1, local copies, waits for them, and re-layouts, per_device(): picked = near_panel[near_slot]  11.7 us
    all_to_all x1, blocking collectives, per_device(): lax.all_to_all(wanted.reshape(devices, 1), 'rows', split_axis=0, concat_a...  9.31 us
    another operation x2, other arithmetic, per_device(): jnp.stack(stripes).reshape(heavy_count * blocks_dev, block_rows, feat_dev)  7.9 us
  transfers between devices with their start and end apart: 2, of which 2 were waited for; matrix products, arithmetic and copies ran while one was open for 7% of the time, Pallas kernels for 0%

commit v1 on v0

--- a/solution.py
+++ b/solution.py
@@ -8,7 +8,7 @@
 
 def broadcast(block, axis, owner):
     block = jnp.where(lax.axis_index(axis) == owner, block, jnp.zeros_like(block))
-    return lax.psum(block, axis)
+    return jnp.sum(lax.all_gather(block, axis), axis=0)
 
 
 def per_device(features, norm_gain, row_counts, tile_cols, tile_values):

time: 342 us -> 822 us (2.40)
  waiting for transfers between devices: 194 us -> 649 us
  other arithmetic: 23.2 us -> 48.6 us
    all_gather x0 -> x3, waiting for transfers between devices: none -> 609 us  [broadcast(): return jnp.sum(lax.all_gather(block, axis), axis=0)]
    psum x1 -> x0, waiting for transfers between devices: 158 us -> none  [broadcast(): return lax.psum(block, axis)]
    reduce_sum x0 -> x3, other arithmetic: none -> 25.4 us  [broadcast(): return jnp.sum(lax.all_gather(block, axis), axis=0)]
  transfers between devices with their start and end apart: 2 -> 4, of which waited for: 2 -> 4; matrix products, arithmetic and copies ran while one was open for 7% -> 5% of each run, Pallas kernels for 0% -> 0%
where the time goes in v1:
time: 822 us; the launch traced here: 821 us
  waiting for transfers between devices  649 us (79%)
  local copies, waits for them, and re-layouts  50.5 us (6%)
  other arithmetic  48.6 us (6%)
  blocking collectives  28.1 us (3%)
  matrix products  26.4 us (3%)
  between operations  15.2 us (2%)
    all_gather x3, waiting for transfers between devices, broadcast(): return jnp.sum(lax.all_gather(block, axis), axis=0)  609 us
    all_to_all x1, waiting for transfers between devices, per_device(): lax.all_to_all(outgoing, 'rows', split_axis=0, concat_axis=0, tiled=True)  38.3 us
    reduce_sum x3, other arithmetic, broadcast(): return jnp.sum(lax.all_gather(block, axis), axis=0)  25.4 us
    unnamed x11, local copies, waits for them, and re-layouts  23.3 us
  transfers between devices with their start and end apart: 4, of which 4 were waited for; matrix products, arithmetic and copies ran while one was open for 5% of the time, Pallas kernels for 0%

profile of v1, /device:TPU:0, one launch (start us, length us, event | category | flops | bytes accessed | tf_op | source)
XLA Modules:
  0.0 821.3 jit_solution(16775534348973195489)
XLA Ops:
  8.2 13.1 %pmax.7 = s32[8]{0:T(128)S(1)} all-reduce(s32[8]{0:T(128)S(1)} %compare_convert_fusion), channel_id=1, replica_groups=mesh['rows'=8,'feat'=4] {'rows'}, use_global_device_ids=true, to_apply=%region_4.5 | all-reduce | flops 8 | bytes 64 | tf_op jit(solution)/shard_map/pmax | solution.py:35
  24.2 4.6 broadcast_select_fusion.2
  32.6 9.1 %all_to_all.14 = s32[8,1,1]{2,1,0:T(1,128)S(1)} all-to-all(s32[8,1,1]{2,1,0:T(1,128)S(1)} %copy.13), channel_id=1, replica_groups=mesh['rows'=8,'feat'=4] {'rows'}, dimensions={0} | all-to-all | bytes 64 | tf_op jit(solution)/shard_map/all_to_all | solution.py:57
  44.0 3.6 all-to-all-start.1
  47.8 2.6 sort.17
  50.4 5.9 gather_fusion.1
  57.7 4.0 gather_fusion.5
  63.7 38.3 %all-to-all-done.1 = f32[8,128,256]{2,1,0:T(8,128)S(1)} async-done(((f32[8,128,256]{2,1,0:T(8,128)}), f32[8,128,256]{2,1,0:T(8,128)S(1)}, u32[]{:S(2)}, u32[]{:S(2)}) %all-to-all-start.1) | async-done | bytes 1048608 | tf_op jit(solution)/shard_map/all_to_all | solution.py:76
  102.1 2.1 convolution_bitcast_fusion
  105.8 170.7 %all-gather.9.cloned.1.call-done = f32[16384,256]{1,0:T(8,128)} async-done(((f32[2048,256]{1,0:T(8,128)}), f32[16384,256]{1,0:T(8,128)}) %all-gather.9.cloned.1.call-update) | async-done | bytes 16777232 | tf_op jit(solution)/shard_map/all_gather | solution.py:11
  276.5 8.5 %reduce_sum.96 = f32[2048,256]{1,0:T(8,128)} reduce(f32[8,2048,256]{2,1,0:T(8,128)} %bitcast.50, f32[]{:T(128)} %constant.66.clone.1), dimensions={0}, to_apply=%region_12.13 | reduce | flops 3670016 | bytes 18874372 | tf_op jit(solution)/shard_map/reduce_sum | solution.py:11
  285.0 219.1 %all-gather.11.cloned.1.call-done = f32[16384,256]{1,0:T(8,128)} async-done(((f32[2048,256]{1,0:T(8,128)}), f32[16384,256]{1,0:T(8,128)}) %all-gather.11.cloned.1.call-update) | async-done | bytes 16777232 | tf_op jit(solution)/shard_map/all_gather | solution.py:11
  504.1 8.5 %reduce_sum.97 = f32[2048,256]{1,0:T(8,128)} reduce(f32[8,2048,256]{2,1,0:T(8,128)} %bitcast.51, f32[]{:T(128)} %constant.66.clone.1), dimensions={0}, to_apply=%region_13.14 | reduce | flops 3670016 | bytes 18874372 | tf_op jit(solution)/shard_map/reduce_sum | solution.py:11
  512.6 219.2 %all-gather.7.cloned.1.call-done = f32[16384,256]{1,0:T(8,128)} async-done(((f32[2048,256]{1,0:T(8,128)}), f32[16384,256]{1,0:T(8,128)}) %all-gather.7.cloned.1.call-update) | async-done | bytes 16777232 | tf_op jit(solution)/shard_map/all_gather | solution.py:11
  731.8 8.5 %reduce_sum.95 = f32[2048,256]{1,0:T(8,128)} reduce(f32[8,2048,256]{2,1,0:T(8,128)} %bitcast.52, f32[]{:T(128)} %constant.66.clone.1), dimensions={0}, to_apply=%region_11.12 | reduce | flops 3670016 | bytes 18874372 | tf_op jit(solution)/shard_map/reduce_sum | solution.py:11
  740.2 3.3 pad_maximum_fusion.1
  743.5 3.9 pad_maximum_fusion
  747.4 11.7 %gather_fusion.3 = f32[83,128,256]{2,1,0:T(8,128)} fusion(f32[64,128,256]{2,1,0:T(8,128)} %pad_maximum_fusion, s32[1024]{0:T(1024)S(1)} %pad_clamp_fusion.2), kind=kCustom, calls=%fused_computation.3 | custom fusion | bytes 21758284 | tf_op jit(solution)/shard_map/gather | solution.py:91
  759.0 15.0 %fusion.22 = f32[83,128,256]{2,1,0:T(8,128)S(1)} fusion(f32[83,128,128]{2,1,0:T(8,128)} %gather_fusion.1, f32[83,128,256]{2,1,0:T(8,128)} %gather_fusion.3), kind=kOutput, calls=%fused_computation.77 | convolution fusion | flops 4177526784 | bytes 27197440 | tf_op jit(solution)/shard_map/tij,tjf->tif/dot_general | solution.py:92
  774.1 5.5 pad.15
  779.6 16.1 %copy.14 = f32[11,8,128,256]{3,1,2,0:T(8,128)} copy(f32[11,8,128,256]{3,2,1,0:T(8,128)} %bitcast.47) | data formatting | bytes 23068672
  795.7 6.9 fusion.3
  802.6 2.4 convolution_add_fusion
  807.1 6.0 psum.7
  (55 shorter events, 17.7 us)
Async XLA Ops:
  6.5 270.0 %all-gather.9.cloned.1.call-start = ((), (), s32[]{:S(2)}) async-start(), calls=%async_computation.3 | async-start | bytes 18874368 | tf_op jit(solution)/shard_map/all_gather | solution.py:11
  28.8 18.8 %copy-start.3 = (s32[1,16]{1,0:T(1,128)S(1)}, s32[1,16]{1,0:T(1,128)}, u32[]{:S(2)}) copy-start(s32[1,16]{1,0:T(1,128)} %param.7) | copy-start | bytes 196
  28.8 475.3 %all-gather.11.cloned.1.call-start = ((), (), s32[]{:S(2)}) async-start(), calls=%async_computation.4 | async-start | bytes 18874368 | tf_op jit(solution)/shard_map/all_gather | solution.py:11
  29.5 702.2 %all-gather.7.cloned.1.call-start = ((), (), s32[]{:S(2)}) async-start(), calls=%async_computation.2 | async-start | bytes 18874368 | tf_op jit(solution)/shard_map/all_gather | solution.py:11
  44.0 58.1 %all-to-all-start.1 = ((f32[8,128,256]{2,1,0:T(8,128)}), f32[8,128,256]{2,1,0:T(8,128)S(1)}, u32[]{:S(2)}, u32[]{:S(2)}) async-start(f32[8,128,256]{2,1,0:T(8,128)} %broadcast_select_fusion.3), calls=%async_computation.1 | async-start | bytes 2097152 | tf_op jit(solution)/shard_map/all_to_all | solution.py:76
  50.4 12.1 %copy-start.1 = (s32[86]{0:T(128)S(1)}, s32[86]{0:T(128)}, u32[]{:S(2)}) copy-start(s32[86]{0:T(128)} %param.8) | copy-start | bytes 1036
  795.7 6.9 copy-start
  802.6 10.4 %copy-start.2 = (f32[256]{0:T(256)S(1)}, f32[256]{0:T(256)}, u32[]{:S(2)}) copy-start(f32[256]{0:T(256)} %param.6) | copy-start | bytes 3076
Sparse Core Ops, SparseCore 0:
  28.9 247.5 all-gather.8
  278.6 225.4 all-gather.10
  506.3 225.4 all-gather.6
